TPU v7x, 32 devices: a whole 2x2x4 slice. The times are simulated.
32 devices in a mesh: section: 4 (over z), dp: 2 (over x), tensor: 4 (over y, core).
Axes of the slice: x: 2, y: 2, z: 4, core: 2. Of those that a mesh axis runs over, the one named last changes fastest.
Arguments:
- sent: bfloat16 [8, 384, 6144], P('section', 'dp', 'tensor'), may hold values from -6 to 6
- stashed_inputs: bfloat16 [16, 96, 6144], P('section', 'dp', 'tensor'), may hold values from -6 to 6
- table: int32 [4, 4], P('section'), may hold values from 0 to 3, each once within a row
- embedded: bfloat16 [384, 6144], P('dp', 'tensor'), may hold values from -6 to 6
- loss_gradient: bfloat16 [384, 6144], P('dp', 'tensor'), may hold values from -6 to 6
- weight: bfloat16 [4, 6144, 6144], P('section', None, 'tensor'), may hold values from -0.078125 to 0.078125
- adapter_down_weight: bfloat16 [4, 6144, 128], P('section'), may hold values from -0.078125 to 0.078125
- adapter_up_weight: bfloat16 [4, 128, 6144], P('section', None, 'tensor'), may hold values from -0.5 to 0.5
Outputs:
- forward_output: bfloat16 [4, 384, 6144], P('section', 'dp', 'tensor')
- backward_output: bfloat16 [4, 384, 6144], P('section', 'dp', 'tensor')
- down_gradient: bfloat16 [4, 6144, 128], P('section', 'tensor')
- up_gradient: bfloat16 [4, 128, 6144], P('section', None, 'tensor')
Inputs may be any that keep to these rules, and one draw needn't show every extreme that they name: Each row of table is a permutation of 0 to 3.
All inputs are finite; a program needn't handle non-finite values.
Results may differ from a plain program's by a relative error of at most 0.019.
Values may be sent and summed in bfloat16 or wider, within the bound.
A program may use at most 64 MiB of HBM per device.

v0:
```python
import functools

import jax
import jax.numpy as jnp
from jax import lax
from jax.experimental import pallas as pl
from jax.experimental.pallas import tpu as pltpu
from jax.sharding import PartitionSpec as P

coef = 0.7978845608028654


def shifted(block, axis, distance):
    devices = range(lax.axis_size(axis))
    route = [(i - distance, i) for i in devices if i - distance in devices]
    return lax.ppermute(block, axis, route)


def gelu_pair(u):
    inner = coef * (u + 0.044715 * u * u * u)
    tanh_v = jnp.tanh(inner)
    value = 0.5 * u * (1.0 + tanh_v)
    slope = 0.5 * (1.0 + tanh_v) + 0.5 * u * (1.0 - tanh_v * tanh_v) * coef * (
        1.0 + 3.0 * 0.044715 * u * u
    )
    return (value, slope)


def on_device(
    sent,
    stashed_inputs,
    table,
    embedded,
    loss_gradient,
    weight,
    adapter_down_weight,
    adapter_up_weight,
):
    section = lax.axis_index("section")
    sections = lax.axis_size("section")
    w_section = weight[0]
    down_matrix = adapter_down_weight[0]
    up_matrix = adapter_up_weight[0]
    below = shifted(sent[1], "section", 1)
    above = shifted(sent[0], "section", -1)
    forward_input = jnp.where(section == 0, embedded, below)
    incoming_gradient = jnp.where(section == sections - 1, loss_gradient, above)
    order = jnp.argsort(table[0])
    arranged = jnp.take(stashed_inputs, order, axis=0)
    fetched = lax.all_to_all(arranged, "section", split_axis=0, concat_axis=0, tiled=True)
    backward_input = fetched.reshape(-1, fetched.shape[-1])
    full_a, full_b = (
        lax.all_gather(forward_input, "tensor", axis=1, tiled=True),
        lax.all_gather(backward_input, "tensor", axis=1, tiled=True),
    )
    main_a = jnp.dot(full_a, w_section, preferred_element_type=jnp.float32)
    h_a = jnp.dot(full_a, down_matrix, preferred_element_type=jnp.float32).astype(jnp.bfloat16)
    u_a = main_a + jnp.dot(h_a, up_matrix, preferred_element_type=jnp.float32)
    value_a, unused = gelu_pair(u_a)
    forward_output = (forward_input.astype(jnp.float32) + value_a).astype(jnp.bfloat16)
    h_b = jnp.dot(full_b, down_matrix, preferred_element_type=jnp.float32).astype(jnp.bfloat16)
    u_b = jnp.dot(full_b, w_section, preferred_element_type=jnp.float32) + jnp.dot(
        h_b, up_matrix, preferred_element_type=jnp.float32
    )
    unused_b, slope_b = gelu_pair(u_b)
    scaled = (incoming_gradient.astype(jnp.float32) * slope_b).astype(jnp.bfloat16)
    low_part = lax.dot_general(
        scaled, up_matrix, (((1,), (1,)), ((), ())), preferred_element_type=jnp.float32
    )
    low_piece = low_part.astype(jnp.bfloat16)
    partial_value = lax.dot_general(
        scaled, w_section, (((1,), (1,)), ((), ())), preferred_element_type=jnp.float32
    )
    partial_value = partial_value + lax.dot_general(
        low_piece, down_matrix, (((1,), (1,)), ((), ())), preferred_element_type=jnp.float32
    )
    input_grad = lax.psum_scatter(
        partial_value.astype(jnp.bfloat16), "tensor", scatter_dimension=1, tiled=True
    ).astype(jnp.float32)
    backward_output = (incoming_gradient.astype(jnp.float32) + input_grad).astype(jnp.bfloat16)
    low_grad = lax.psum(low_part.astype(jnp.bfloat16), "tensor")
    down_term = lax.dot_general(
        backward_input, low_grad, (((0,), (0,)), ((), ())), preferred_element_type=jnp.float32
    )
    up_term = lax.dot_general(
        h_b, scaled, (((0,), (0,)), ((), ())), preferred_element_type=jnp.float32
    )
    down_sum, up_sum = (
        lax.psum(down_term.astype(jnp.bfloat16), "dp").astype(jnp.float32),
        lax.psum(up_term.astype(jnp.bfloat16), "dp").astype(jnp.float32),
    )
    down_gradient = down_sum.astype(jnp.bfloat16)
    up_gradient = up_sum.astype(jnp.bfloat16)
    return (forward_output[None], backward_output[None], down_gradient[None], up_gradient[None])


F32 = jnp.float32
BF16 = jnp.bfloat16
MESH = pl.DeviceIdType.MESH


def dot_nn(a, b):
    return lax.dot_general(a, b, (((1,), (0,)), ((), ())), preferred_element_type=F32)


def dot_nt(a, b):
    return lax.dot_general(a, b, (((1,), (1,)), ((), ())), preferred_element_type=F32)


def dot_tn(a, b):
    return lax.dot_general(a, b, (((0,), (0,)), ((), ())), preferred_element_type=F32)


def window_kernel(
    sections, tile,
    sent, stash_hbm, table, embedded, loss, weight, down, up,
    out_f, out_b, out_d, out_u,
    stash_v, w, dn, upv, xa, xb, g, arranged, u, ua, scaled, low, lowr, hb,
    p_send, q_send, o_send, p_recv, q_recv, o_recv, own,
    du_send, du_recv, xo, lg, lg_recv,
    w_sem, d_sem, loc_sem, ex_s, ex_r, az_s, az_r, gz_s, gz_r,
    xo_s, xo_r, bx_s, bx_r, ax_s, ax_r, low_s, low_r, p_s, p_r, q_s, q_r, o_s, o_r, dp_s, dp_r,
):
    S = sections
    s = lax.axis_index("section")
    d = lax.axis_index("dp")
    t = lax.axis_index("tensor")
    t1 = t + 1 - 2 * (t % 2)
    t2 = (t + 2) % 4
    t3 = (t1 + 2) % 4
    rel = [t, t1, t2, t3]
    piece, cols = stash_v.shape[1], stash_v.shape[2]
    rows = S * piece
    tiles = cols // tile
    stash_copy = pltpu.make_async_copy(stash_hbm, stash_v, loc_sem.at[0])
    stash_copy.start()

    def remote(src, dst, ss, rs, **device):
        return pltpu.make_async_remote_copy(
            src_ref=src, dst_ref=dst, send_sem=ss, recv_sem=rs,
            device_id=device, device_id_type=MESH)

    emb_copy = pltpu.make_async_copy(embedded, xa.at[0], loc_sem.at[3])
    loss_copy = pltpu.make_async_copy(loss, g, loc_sem.at[1])
    up_copy = pltpu.make_async_copy(up, upv, loc_sem.at[2])
    w_copies = [pltpu.make_async_copy(weight.at[rel[r]], w.at[r], w_sem.at[r]) for r in range(4)]
    d_copies = [pltpu.make_async_copy(down.at[rel[r]], dn.at[r], d_sem.at[r]) for r in range(4)]

    barrier = pltpu.get_barrier_semaphore()
    for j in range(1, S):
        pl.semaphore_signal(barrier, inc=1, device_id={"section": (s + j) % S}, device_id_type=MESH)
    for r in range(1, 4):
        pl.semaphore_signal(barrier, inc=1, device_id={"tensor": rel[r]}, device_id_type=MESH)
    pl.semaphore_signal(barrier, inc=1, device_id={"dp": 1 - d}, device_id_type=MESH)

    stash_copy.wait()
    for j in range(S):
        dest = (s + j) % S
        k = jnp.int32(0)
        for i in range(S):
            k = jnp.where(table[0, i] == dest, i, k)
        if j == 0:
            xb[0, s] = stash_v[k]
        else:
            arranged[j] = stash_v[k]
    pl.semaphore_wait(barrier, S + 3)

    ex = [None] + [
        remote(arranged.at[j], xb.at[0, s], ex_s.at[j], ex_r.at[j], section=(s + j) % S)
        for j in range(1, S)
    ]
    for j in EX_ORDER(S):
        ex[j].start()

    @pl.when(s == 0)
    def _():
        emb_copy.start()

    @pl.when(s == S - 1)
    def _():
        loss_copy.start()

    for r in range(4):
        d_copies[r].start()
        w_copies[r].start()
    up_copy.start()

    az = [remote(sent.at[1, c], xa.at[0, c], az_s.at[c], az_r.at[c], section=(s + 1) % S) for c in range(S)]
    gz = remote(sent.at[0], g, gz_s.at[0], gz_r.at[0], section=(s + S - 1) % S)

    @pl.when(s < S - 1)
    def _():
        for c in range(S):
            az[c].start()

    @pl.when(s > 0)
    def _():
        gz.start()

    def hops(x, c, sem_s, sem_r, i):
        return (
            remote(x.at[0, c], x.at[1, c], sem_s.at[0, i], sem_r.at[0, i], tensor=t1),
            remote(x.at[0, c], x.at[2, c], sem_s.at[1, i], sem_r.at[1, i], tensor=t2),
            remote(x.at[2, c], x.at[3, c], sem_s.at[2, i], sem_r.at[2, i], tensor=t1),
        )

    b_list = [0] + WAIT_ORDER(S)
    bh = [hops(xb, (s + S - j) % S, bx_s, bx_r, i) for i, j in enumerate(b_list)]
    ah = [hops(xa, c, ax_s, ax_r, c) for c in range(S)]

    xos = [
        remote(xb.at[0, (s + S - j) % S], xo.at[(s + S - j) % S], xo_s.at[i], xo_r.at[i], dp=1 - d)
        for i, j in enumerate(b_list)
    ]

    def b_piece(i):
        j = b_list[i]
        if j:
            src = (s + S - j) % S
            remote(arranged.at[j], xb.at[0, src], ex_s.at[j], ex_r.at[j], section=src).wait_recv()
        bh[i][1].start()
        bh[i][0].start()
        xos[i].start()

    def b_pass(i):
        bh[i][1].wait_recv()
        bh[i][2].start()

    def a_piece(c):
        if c == 0:
            @pl.when(s == 0)
            def _():
                emb_copy.wait()

        @pl.when(s > 0)
        def _():
            az[c].wait_recv()
        ah[c][1].start()
        ah[c][0].start()

    def a_pass(c):
        ah[c][1].wait_recv()
        ah[c][2].start()

    def forward(x, r, acc, first):
        lhs = x.at[r]

        def body(n, carry):
            at = pl.ds(pl.multiple_of(n * tile, tile), tile)
            val = dot_nn(lhs[...].reshape(rows, cols), w[r, :, at])
            if first:
                acc[n] = val
            else:
                acc[n] = acc[n] + val
            return carry
        lax.fori_loop(0, tiles, body, 0)

    def low_of(x, r):
        return dot_nn(x[r].reshape(rows, cols), dn[r])

    for i in range(S):
        b_piece(i)
        if i >= 1:
            b_pass(i - 1)

    d_copies[0].wait()
    w_copies[0].wait()
    forward(xb, 0, u, True)
    h = low_of(xb, 0)
    b_pass(S - 1)
    a_piece(0)
    for i in range(S):
        bh[i][0].wait_recv()
    d_copies[1].wait()
    w_copies[1].wait()
    forward(xb, 1, u, False)
    h = h + low_of(xb, 1)
    a_piece(1)
    d_copies[2].wait()
    w_copies[2].wait()
    forward(xb, 2, u, False)
    h = h + low_of(xb, 2)
    for i in range(S):
        bh[i][2].wait_recv()
    d_copies[3].wait()
    w_copies[3].wait()
    forward(xb, 3, u, False)
    h = h + low_of(xb, 3)
    hb[...] = h.astype(BF16)
    up_copy.wait()

    def slope_body(n, carry):
        at = pl.ds(pl.multiple_of(n * tile, tile), tile)
        unused, slope = gelu_pair(u[n] + dot_nn(hb[...], upv[:, at]))
        u[n] = slope
        return carry
    lax.fori_loop(0, tiles, slope_body, 0)
    a_pass(0)
    for c in range(2, S):
        a_piece(c)
        a_pass(c - 1)

    @pl.when(s == S - 1)
    def _():
        loss_copy.wait()

    @pl.when(s < S - 1)
    def _():
        gz.wait_recv()

    def scale_body(n, carry):
        at = pl.ds(pl.multiple_of(n * tile, tile), tile)
        scaled[:, at] = (g[:, :, at].reshape(rows, tile).astype(F32) * u[n]).astype(BF16)
        return carry
    lax.fori_loop(0, tiles, scale_body, 0)

    low[...] = dot_nt(scaled[...], upv[...]).astype(BF16)
    lows = [None] + [
        remote(low, lowr.at[r], low_s.at[r], low_r.at[r], tensor=rel[r]) for r in range(1, 4)
    ]
    for r in (2, 3, 1):
        lows[r].start()

    def partial(r, n):
        at = pl.ds(pl.multiple_of(n * tile, tile), tile)
        return dot_nt(scaled[...], w[r, at, :]) + dot_nt(low[...], dn[r, at, :])

    def p_copy(n):
        return remote(p_send.at[n], p_recv.at[n], p_s.at[n], p_r.at[n], tensor=t1)

    def q_copy(n):
        return remote(q_send.at[n], q_recv.at[n], q_s.at[n], q_r.at[n], tensor=t2)

    def o_copy(n):
        return remote(o_send.at[n], o_recv.at[n], o_s.at[n], o_r.at[n], tensor=t1)

    def p_body(n, carry):
        p_send[n] = partial(3, n).astype(BF16)
        p_copy(n).start()
        return carry
    lax.fori_loop(0, tiles, p_body, 0)

    def up_body(n, carry):
        at = pl.ds(pl.multiple_of(n * tile, tile), tile)
        du_send[:, at] = dot_tn(hb[...], scaled[:, at]).astype(BF16)
        return carry
    lax.fori_loop(0, tiles, up_body, 0)
    du = remote(du_send, du_recv, dp_s.at[0], dp_r.at[0], dp=1 - d)
    du.start()

    def q_body(n, carry):
        mine = partial(2, n)
        p_copy(n).wait_recv()
        q_send[n] = (mine + p_recv[n].astype(F32)).astype(BF16)
        q_copy(n).start()
        return carry
    lax.fori_loop(0, tiles, q_body, 0)
    a_pass(S - 1)

    total = low[...].astype(F32)
    for r in range(1, 4):
        lows[r].wait_recv()
        total = total + lowr[r].astype(F32)
    lg[...] = total.astype(BF16)
    dd = remote(lg, lg_recv, dp_s.at[1], dp_r.at[1], dp=1 - d)
    dd.start()

    def o_body(n, carry):
        o_send[n] = partial(1, n).astype(BF16)
        o_copy(n).start()
        return carry
    lax.fori_loop(0, tiles, o_body, 0)

    def own_body(n, carry):
        own[n] = partial(0, n)
        return carry
    lax.fori_loop(0, tiles, own_body, 0)

    forward(xa, 0, ua, True)
    h = low_of(xa, 0)
    for c in range(S):
        ah[c][0].wait_recv()
    forward(xa, 1, ua, False)
    h = h + low_of(xa, 1)
    forward(xa, 2, ua, False)
    h = h + low_of(xa, 2)
    for c in range(S):
        ah[c][2].wait_recv()
    forward(xa, 3, ua, False)
    h = h + low_of(xa, 3)
    ha = h.astype(BF16)
    hb2 = lowr.at[1]
    hb2[...] = ha

    def out_body(n, carry):
        at = pl.ds(pl.multiple_of(n * tile, tile), tile)
        value, unused = gelu_pair(ua[n] + dot_nn(lowr[1], upv[:, at]))
        base = xa[0, :, :, at].reshape(rows, tile).astype(F32)
        out_f[:, at] = (base + value).astype(BF16)
        return carry
    lax.fori_loop(0, tiles, out_body, 0)

    du.wait_recv()
    out_u[...] = (du_send[...].astype(F32) + du_recv[...].astype(F32)).astype(BF16)

    for i in range(S):
        xos[i].wait_recv()
    dd.wait_recv()
    here = dot_tn(xb[0].reshape(rows, cols), lg[...]).astype(BF16)
    there = dot_tn(xo[...].reshape(rows, cols), lg_recv[...]).astype(BF16)
    out_d[...] = (here.astype(F32) + there.astype(F32)).astype(BF16)

    for n in range(tiles):
        o_copy(n).wait_recv()
        q_copy(n).wait_recv()
        at = pl.ds(n * tile, tile)
        total = own[n] + o_recv[n].astype(F32) + q_recv[n].astype(F32)
        out_b[:, at] = (g[:, :, at].reshape(rows, tile).astype(F32) + total).astype(BF16)

    for j in range(1, S):
        ex[j].wait_send()

    @pl.when(s < S - 1)
    def _():
        for c in range(S):
            az[c].wait_send()

    @pl.when(s > 0)
    def _():
        gz.wait_send()
    for i in range(S):
        xos[i].wait_send()
        for hop in range(3):
            bh[i][hop].wait_send()
            ah[i][hop].wait_send()
    for r in range(1, 4):
        lows[r].wait_send()
    for n in range(tiles):
        p_copy(n).wait_send()
        q_copy(n).wait_send()
        o_copy(n).wait_send()
    du.wait_send()
    dd.wait_send()


def EX_ORDER(S):
    return sorted(range(1, S), key=lambda j: (-min(j, S - j), j))


def WAIT_ORDER(S):
    return sorted(range(1, S), key=lambda j: (min(j, S - j), j))


def fused_on_device(sent, stash, table, embedded, loss, weight, down, up):
    S = lax.axis_size("section")
    piece, cols = stash.shape[1], stash.shape[2]
    rows, rank = S * piece, up.shape[1]
    tile = next(k for k in (768, 512, 256, 128) if cols % k == 0)
    tiles = cols // tile
    any_space = pl.BlockSpec(memory_space=pl.ANY)
    hbm = pl.BlockSpec(memory_space=pltpu.HBM)
    vmem = pl.BlockSpec(memory_space=pltpu.VMEM)
    smem = pl.BlockSpec(memory_space=pltpu.SMEM)
    V = pltpu.VMEM
    dma = lambda *shape: pltpu.SemaphoreType.DMA(shape)
    block = (tiles, rows, tile)
    outs = pl.pallas_call(
        functools.partial(window_kernel, S, tile),
        out_shape=(
            jax.ShapeDtypeStruct((rows, cols), BF16),
            jax.ShapeDtypeStruct((rows, cols), BF16),
            jax.ShapeDtypeStruct((cols, rank), BF16),
            jax.ShapeDtypeStruct((rank, cols), BF16),
        ),
        in_specs=[hbm, hbm, smem, hbm, hbm, hbm, hbm, hbm],
        out_specs=(vmem,) * 4,
        scratch_shapes=[
            V((S, piece, cols), BF16), V((4, cols, cols), BF16), V((4, cols, rank), BF16), V((rank, cols), BF16),
            V((4, S, piece, cols), BF16), V((4, S, piece, cols), BF16),
            V((S, piece, cols), BF16), V((S, piece, cols), BF16),
            V(block, F32), V(block, F32), V((rows, cols), BF16),
            V((rows, rank), BF16), V((4, rows, rank), BF16), V((rows, rank), BF16),
            V(block, BF16), V(block, BF16), V(block, BF16),
            V(block, BF16), V(block, BF16), V(block, BF16), V(block, F32),
            V((rank, cols), BF16), V((rank, cols), BF16),
            V((S, piece, cols), BF16), V((rows, rank), BF16), V((rows, rank), BF16),
            dma(4), dma(4), dma(4), dma(S), dma(S), dma(S), dma(S), dma(1), dma(1), dma(S), dma(S),
            dma(3, S), dma(3, S), dma(3, S), dma(3, S), dma(4), dma(4),
            dma(tiles), dma(tiles), dma(tiles), dma(tiles), dma(tiles), dma(tiles),
            dma(2), dma(2),
        ],
        compiler_params=pltpu.CompilerParams(
            collective_id=0, has_side_effects=True, vmem_limit_bytes=60 * 1024 * 1024),
    )(
        sent.reshape(2, S, piece, cols), stash, table,
        embedded.reshape(S, piece, cols), loss.reshape(S, piece, cols),
        weight.reshape(4, cols, cols), down.reshape(4, cols, rank), up[0],
    )
    return tuple(o[None] for o in outs)


def solution(mesh):
    placed = (
        P("section", "dp", "tensor"),
        P("section", "dp", "tensor"),
        P("section", None),
        P("dp", "tensor"),
        P("dp", "tensor"),
        P("section", None, "tensor"),
        P("section", None, None),
        P("section", None, "tensor"),
    )
    def program(*args):
        rows = args[1].shape[1] // mesh.shape["dp"]
        cols = args[1].shape[2] // mesh.shape["tensor"]
        fits = (
            mesh.shape["tensor"] == 4 and mesh.shape["dp"] == 2
            and rows % 16 == 0 and cols % 128 == 0
        )
        return sharded(fused_on_device if fits else on_device)(*args)

    def sharded(body):
      return jax.shard_map(
        body,
        mesh=mesh,
        in_specs=placed,
        out_specs=(
            P("section", "dp", "tensor"),
            P("section", "dp", "tensor"),
            P("section", "tensor", None),
            P("section", None, "tensor"),
        ),
        check_vma=False,
    )

    return program
```

profile of v0, /device:TPU:22, one launch (start us, length us, event | category | flops | bytes accessed | tf_op | source)
XLA Modules:
  0.0 65.3 jit_solution(1003119364642946558)
XLA Ops:
  0.6 60.3 %shard_map.111 = (bf16[192,1536]{1,0:T(8,128)(2,1)}, bf16[192,1536]{1,0:T(8,128)(2,1)}, bf16[1536,128]{1,0:T(8,128)(2,1)}, bf16[128,1536]{1,0:T(8,128)(2,1)}) custom-call(bf16[2,4,48,1536]{3,2,1,0:T(8,128)(2,1)} %bitcast.12, bf16[4,48,1536]{2,1,0:T(8,128)(2,1)} %stash_hbm.1, s32[1,4]{1,0:T(1,128)} %table.1, bf16[4,48,1536]{2,1,0:T(8,128)(2,1)} %bitcast.13, ...), custom_call_target="tpu_custom_call" | custom-call | tf_op jit(solution)/shard_map/pallas_call | solution.py:467
  60.9 0.0 copy-start
  60.9 0.0 copy-start.2
  60.9 0.0 copy-start.1
  60.9 2.0 %copy.16 = bf16[1,192,1536]{2,1,0:T(8,128)(2,1)} copy(bf16[1,192,1536]{2,1,0:T(8,128)(2,1)} %bitcast.16) | data formatting | bytes 1179648
  63.0 0.0 copy-done
  63.0 0.8 %copy.17 = bf16[1,192,1536]{2,1,0:T(8,128)(2,1)} copy(bf16[1,192,1536]{2,1,0:T(8,128)(2,1)S(1)} %bitcast.15) | data formatting | bytes 1179648
  63.8 0.0 copy-done.2
  63.8 0.7 %copy.18 = bf16[1,1536,128]{2,1,0:T(8,128)(2,1)} copy(bf16[1,1536,128]{2,1,0:T(8,128)(2,1)S(1)} %bitcast.18) | data formatting | bytes 786432
  64.5 0.0 copy-done.1
  64.5 0.7 %copy.19 = bf16[1,128,1536]{2,1,0:T(8,128)(2,1)} copy(bf16[1,128,1536]{2,1,0:T(8,128)(2,1)S(1)} %bitcast.17) | data formatting | bytes 786432
Async XLA Ops:
  60.9 2.1 %copy-start = (bf16[192,1536]{1,0:T(8,128)(2,1)S(1)}, bf16[192,1536]{1,0:T(8,128)(2,1)}, u32[]{:S(2)}) copy-start(bf16[192,1536]{1,0:T(8,128)(2,1)} %get-tuple-element.9) | copy-start | bytes 1769476
  60.9 2.9 %copy-start.2 = (bf16[1536,128]{1,0:T(8,128)(2,1)S(1)}, bf16[1536,128]{1,0:T(8,128)(2,1)}, u32[]{:S(2)}) copy-start(bf16[1536,128]{1,0:T(8,128)(2,1)} %get-tuple-element.10) | copy-start | bytes 1179652
  60.9 3.6 %copy-start.1 = (bf16[128,1536]{1,0:T(8,128)(2,1)S(1)}, bf16[128,1536]{1,0:T(8,128)(2,1)}, u32[]{:S(2)}) copy-start(bf16[128,1536]{1,0:T(8,128)(2,1)} %get-tuple-element.11) | copy-start | bytes 1179652
where the time goes:
time: 65.5 us; the launch traced here: 65.3 us
  Pallas kernels  60.3 us (92%)
  local copies, waits for them, and re-layouts  4.34 us (7%)
  between operations  0.67 us (1%)
    pallas_call x1, Pallas kernels, fused_on_device(): pl.pallas_call(functools.partial(window_kernel, S, tile), out_shape=(jax....  60.3 us
    unnamed x10, local copies, waits for them, and re-layouts  4.34 us

commit v1 on v0

v1 whole, which is shorter than its diff:
```python
import functools

import jax
import jax.numpy as jnp
from jax import lax
from jax.experimental import pallas as pl
from jax.experimental.pallas import tpu as pltpu
from jax.sharding import PartitionSpec as P

coef = 0.7978845608028654


def shifted(block, axis, distance):
    devices = range(lax.axis_size(axis))
    route = [(i - distance, i) for i in devices if i - distance in devices]
    return lax.ppermute(block, axis, route)


def gelu_pair(u):
    inner = coef * (u + 0.044715 * u * u * u)
    tanh_v = jnp.tanh(inner)
    value = 0.5 * u * (1.0 + tanh_v)
    slope = 0.5 * (1.0 + tanh_v) + 0.5 * u * (1.0 - tanh_v * tanh_v) * coef * (
        1.0 + 3.0 * 0.044715 * u * u
    )
    return (value, slope)


def on_device(
    sent,
    stashed_inputs,
    table,
    embedded,
    loss_gradient,
    weight,
    adapter_down_weight,
    adapter_up_weight,
):
    section = lax.axis_index("section")
    sections = lax.axis_size("section")
    w_section = weight[0]
    down_matrix = adapter_down_weight[0]
    up_matrix = adapter_up_weight[0]
    below = shifted(sent[1], "section", 1)
    above = shifted(sent[0], "section", -1)
    forward_input = jnp.where(section == 0, embedded, below)
    incoming_gradient = jnp.where(section == sections - 1, loss_gradient, above)
    order = jnp.argsort(table[0])
    arranged = jnp.take(stashed_inputs, order, axis=0)
    fetched = lax.all_to_all(arranged, "section", split_axis=0, concat_axis=0, tiled=True)
    backward_input = fetched.reshape(-1, fetched.shape[-1])
    full_a, full_b = (
        lax.all_gather(forward_input, "tensor", axis=1, tiled=True),
        lax.all_gather(backward_input, "tensor", axis=1, tiled=True),
    )
    main_a = jnp.dot(full_a, w_section, preferred_element_type=jnp.float32)
    h_a = jnp.dot(full_a, down_matrix, preferred_element_type=jnp.float32).astype(jnp.bfloat16)
    u_a = main_a + jnp.dot(h_a, up_matrix, preferred_element_type=jnp.float32)
    value_a, unused = gelu_pair(u_a)
    forward_output = (forward_input.astype(jnp.float32) + value_a).astype(jnp.bfloat16)
    h_b = jnp.dot(full_b, down_matrix, preferred_element_type=jnp.float32).astype(jnp.bfloat16)
    u_b = jnp.dot(full_b, w_section, preferred_element_type=jnp.float32) + jnp.dot(
        h_b, up_matrix, preferred_element_type=jnp.float32
    )
    unused_b, slope_b = gelu_pair(u_b)
    scaled = (incoming_gradient.astype(jnp.float32) * slope_b).astype(jnp.bfloat16)
    low_part = lax.dot_general(
        scaled, up_matrix, (((1,), (1,)), ((), ())), preferred_element_type=jnp.float32
    )
    low_piece = low_part.astype(jnp.bfloat16)
    partial_value = lax.dot_general(
        scaled, w_section, (((1,), (1,)), ((), ())), preferred_element_type=jnp.float32
    )
    partial_value = partial_value + lax.dot_general(
        low_piece, down_matrix, (((1,), (1,)), ((), ())), preferred_element_type=jnp.float32
    )
    input_grad = lax.psum_scatter(
        partial_value.astype(jnp.bfloat16), "tensor", scatter_dimension=1, tiled=True
    ).astype(jnp.float32)
    backward_output = (incoming_gradient.astype(jnp.float32) + input_grad).astype(jnp.bfloat16)
    low_grad = lax.psum(low_part.astype(jnp.bfloat16), "tensor")
    down_term = lax.dot_general(
        backward_input, low_grad, (((0,), (0,)), ((), ())), preferred_element_type=jnp.float32
    )
    up_term = lax.dot_general(
        h_b, scaled, (((0,), (0,)), ((), ())), preferred_element_type=jnp.float32
    )
    down_sum, up_sum = (
        lax.psum(down_term.astype(jnp.bfloat16), "dp").astype(jnp.float32),
        lax.psum(up_term.astype(jnp.bfloat16), "dp").astype(jnp.float32),
    )
    down_gradient = down_sum.astype(jnp.bfloat16)
    up_gradient = up_sum.astype(jnp.bfloat16)
    return (forward_output[None], backward_output[None], down_gradient[None], up_gradient[None])


F32 = jnp.float32
BF16 = jnp.bfloat16
MESH = pl.DeviceIdType.MESH


def dot_nn(a, b):
    return lax.dot_general(a, b, (((1,), (0,)), ((), ())), preferred_element_type=F32)


def dot_nt(a, b):
    return lax.dot_general(a, b, (((1,), (1,)), ((), ())), preferred_element_type=F32)


def dot_tn(a, b):
    return lax.dot_general(a, b, (((0,), (0,)), ((), ())), preferred_element_type=F32)


def stash_order(s, S):
    return sorted(range(S), key=lambda k: (abs(k - s), k))


def link_order(s, S):
    b = [("b", k) for k in stash_order(s, S)]
    a = [("a", c) for c in range(S)]
    if s == 0:
        mixed = [b[0]]
        for k in range(1, S):
            mixed += [a[k - 1], b[k]]
        return mixed + a[S - 1:]
    if s == S - 1:
        return b[:2] + a[:S - 1] + b[2:] + a[S - 1:]
    return b + a


def up_order(s, S):
    b = [("b", k) for k in range(s + 1, S)]
    a = [("a", c) for c in range(S)] if s < S - 1 else []
    if 0 < s < S - 2:
        return b[:1] + a[:2] + b[1:] + a[2:]
    return b + a


def relay_slots(s, S):
    order = link_order(s, S)
    last_b = max(i for i, item in enumerate(order) if item[0] == "b")
    slots = [[], [], [], []]
    for i in range(last_b + 1):
        slots[0].append(("p", order[i]))
        if i:
            slots[0].append(("q", order[i - 1]))
    rest = order[last_b + 1:]
    now = len(rest) if s == 0 else 1
    slots[1] += [("p", item) for item in rest[:now]]
    slots[1].append(("q", order[last_b]))
    sent = rest[:now]
    late = []
    for item in rest[now:]:
        if 0 < s < S - 1 and s != 1 and item == rest[-1]:
            late.append(item)
            continue
        slots[2].append(("p", item))
        slots[2].append(("q", sent.pop(0)))
        sent.append(item)
    slots[3] += [("p", item) for item in late]
    tail = [("q", item) for item in sent + late]
    return slots + [tail]


def window_kernel(
    sections, tile, part,
    sent, stash_hbm, table, embedded, loss, weight, down, up,
    out_f, out_b, out_d, out_u,
    stash_v, w, dn, upv, xa, xb, g, arranged, u, ua, scaled, low, low_in, pair, pair_in, lg, lg_in, hb, ha,
    p_send, q_send, o_send, p_recv, q_recv, o_recv, own,
    du_send, du_recv, xo,
    w_sem, d_sem, loc_sem, ex_s, ex_r, az_s, az_r, gz_s, gz_r,
    xo_s, xo_r, y_s, y_r, c_s, c_r, f_s, f_r, low_s, low_r, p_s, p_r, q_s, q_r, o_s, o_r, dp_s, dp_r,
):
    S = sections
    s = lax.axis_index("section")
    d = lax.axis_index("dp")
    t = lax.axis_index("tensor")
    t1 = t + 1 - 2 * (t % 2)
    t2 = (t + 2) % 4
    t3 = (t1 + 2) % 4
    rel = [t, t1, t2, t3]
    piece, cols = stash_v.shape[1], stash_v.shape[2]
    rows = S * piece
    tiles = cols // tile
    parts = cols // part
    stash_copy = pltpu.make_async_copy(stash_hbm, stash_v, loc_sem.at[0])
    stash_copy.start()

    def remote(src, dst, ss, rs, **device):
        return pltpu.make_async_remote_copy(
            src_ref=src, dst_ref=dst, send_sem=ss, recv_sem=rs,
            device_id=device, device_id_type=MESH)

    emb_copy = pltpu.make_async_copy(embedded, xa.at[0], loc_sem.at[3])
    loss_copy = pltpu.make_async_copy(loss, g, loc_sem.at[1])
    up_copy = pltpu.make_async_copy(up, upv, loc_sem.at[2])
    w_copies = [pltpu.make_async_copy(weight.at[rel[r]], w.at[r], w_sem.at[r]) for r in range(4)]
    d_copies = [pltpu.make_async_copy(down.at[rel[r]], dn.at[r], d_sem.at[r]) for r in range(4)]

    barrier = pltpu.get_barrier_semaphore()
    for j in range(1, S):
        pl.semaphore_signal(barrier, inc=1, device_id={"section": (s + j) % S}, device_id_type=MESH)
    for r in range(1, 4):
        pl.semaphore_signal(barrier, inc=1, device_id={"tensor": rel[r]}, device_id_type=MESH)
    pl.semaphore_signal(barrier, inc=1, device_id={"dp": 1 - d}, device_id_type=MESH)

    @pl.when(s == 0)
    def _():
        emb_copy.start()

    stash_copy.wait()
    for j in range(S):
        dest = (s + j) % S
        k = jnp.int32(0)
        for i in range(S):
            k = jnp.where(table[0, i] == dest, i, k)
        if j == 0:
            xb[0, s] = stash_v[k]
        else:
            arranged[j] = stash_v[k]
    pl.semaphore_wait(barrier, S + 3)

    def ex(v, to):
        return remote(arranged.at[(to - v) % S], xb.at[0, v], ex_s.at[to], ex_r.at[v], section=to)

    def az(v, c):
        return remote(sent.at[1, c], xa.at[0, c], az_s.at[c], az_r.at[c], section=(v + 1) % S)

    gz = remote(sent.at[0], g, gz_s.at[0], gz_r.at[0], section=(s + S - 1) % S)

    def hop_y(item):
        x, k, at = (xb, item[1], item[1]) if item[0] == "b" else (xa, item[1], S + item[1])
        return remote(x.at[0, k], x.at[2, k], y_s.at[at], y_r.at[at], tensor=t2)

    def hop_c(item):
        x, k, at = (xb, item[1], item[1]) if item[0] == "b" else (xa, item[1], S + item[1])
        return remote(x.at[0, k], x.at[1, k], c_s.at[at], c_r.at[at], tensor=t1)

    def hop_f(item):
        x, k, at = (xb, item[1], item[1]) if item[0] == "b" else (xa, item[1], S + item[1])
        return remote(x.at[2, k], x.at[3, k], f_s.at[at], f_r.at[at], tensor=t1)

    def hop_x(k):
        return remote(xb.at[0, k], xo.at[k], xo_s.at[k], xo_r.at[k], dp=1 - d)

    def act(v, step):
        kind, item = step
        if kind == "q":
            hop_y(item).wait_recv()
            hop_f(item).start()
            return
        if item[0] == "b":
            if item[1] != v:
                ex(item[1], v).wait_recv()
        elif v == 0:
            if item[1] == 0:
                emb_copy.wait()
        else:
            az(v - 1, item[1]).wait_recv()
        hop_y(item).start()
        hop_c(item).start()
        if item[0] == "b":
            hop_x(item[1]).start()

    def per_section(run):
        for v in range(S):
            pl.when(s == v)(functools.partial(run, v))

    def relay(slot):
        def run(v):
            for step in relay_slots(v, S)[slot]:
                act(v, step)
        per_section(run)

    def first_sends(v):
        act(v, ("p", ("b", v)))
        for k in range(v - 1, -1, -1):
            ex(v, k).start()
        for kind, k in up_order(v, S):
            if kind == "b":
                ex(v, k).start()
            else:
                az(v, k).start()
        if v > 0:
            gz.start()
        if v == S - 1:
            loss_copy.start()
    per_section(first_sends)

    for r in range(4):
        d_copies[r].start()
        w_copies[r].start()
    up_copy.start()

    def run_rest(v):
        for step in relay_slots(v, S)[0][1:]:
            act(v, step)
    per_section(run_rest)

    def forward(x, r, acc):
        for n in range(tiles):
            val = dot_nn(x[r].reshape(rows, cols), w[r, :, pl.ds(n * tile, tile)])
            acc[n] = val if r == 0 else acc[n] + val

    def low_of(x, r):
        return dot_nn(x[r].reshape(rows, cols), dn[r])

    d_copies[0].wait()
    w_copies[0].wait()
    forward(xb, 0, u)
    h = low_of(xb, 0)
    for k in range(S):
        hop_c(("b", k)).wait_recv()
    d_copies[1].wait()
    w_copies[1].wait()
    forward(xb, 1, u)
    h = h + low_of(xb, 1)
    relay(1)
    d_copies[2].wait()
    w_copies[2].wait()
    forward(xb, 2, u)
    h = h + low_of(xb, 2)
    for k in range(S):
        hop_f(("b", k)).wait_recv()
    d_copies[3].wait()
    w_copies[3].wait()
    forward(xb, 3, u)
    h = h + low_of(xb, 3)
    hb[...] = h.astype(BF16)
    up_copy.wait()

    def slope_body(n, carry):
        at = pl.ds(pl.multiple_of(n * tile, tile), tile)
        unused, slope = gelu_pair(u[n] + dot_nn(hb[...], upv[:, at]))
        u[n] = slope
        return carry
    lax.fori_loop(0, tiles, slope_body, 0)
    relay(2)

    @pl.when(s == S - 1)
    def _():
        loss_copy.wait()

    @pl.when(s < S - 1)
    def _():
        gz.wait_recv()

    def scale_body(n, carry):
        at = pl.ds(pl.multiple_of(n * tile, tile), tile)
        scaled[:, at] = (g[:, :, at].reshape(rows, tile).astype(F32) * u[n]).astype(BF16)
        return carry
    lax.fori_loop(0, tiles, scale_body, 0)

    low_copy = remote(low, low_in, low_s.at[0], low_r.at[0], tensor=t1)
    pair_copy = remote(pair, pair_in, low_s.at[1], low_r.at[1], tensor=t2)

    def partial(r, n):
        return dot_nt(scaled[...], w[r, pl.ds(n * part, part), :])

    def p_copy(n):
        return remote(p_send.at[n], p_recv.at[n], p_s.at[n], p_r.at[n], tensor=t1)

    def q_copy(n):
        return remote(q_send.at[n], q_recv.at[n], q_s.at[n], q_r.at[n], tensor=t2)

    def o_copy(n):
        return remote(o_send.at[n], o_recv.at[n], o_s.at[n], o_r.at[n], tensor=t1)

    def p_step(n):
        p_send[n] = partial(3, n).astype(BF16)
        p_copy(n).start()

    def q_step(n):
        mine = partial(2, n)
        p_copy(n).wait_recv()
        q_send[n] = (mine + p_recv[n].astype(F32)).astype(BF16)
        q_copy(n).start()

    low[...] = dot_nt(scaled[...], upv[...]).astype(BF16)
    low_copy.start()
    p_step(0)
    p_step(1)
    low_copy.wait_recv()
    pair[...] = (low[...].astype(F32) + low_in[...].astype(F32)).astype(BF16)
    pair_copy.start()
    q_step(0)
    relay(3)
    for n in range(2, parts):
        p_step(n)
        q_step(n - 1)
    q_step(parts - 1)

    du_send[...] = dot_tn(hb[...], scaled[...]).astype(BF16)
    pair_copy.wait_recv()
    lg[...] = (pair[...].astype(F32) + pair_in[...].astype(F32)).astype(BF16)
    dd = remote(lg, lg_in, dp_s.at[1], dp_r.at[1], dp=1 - d)
    dd.start()
    du = remote(du_send, du_recv, dp_s.at[0], dp_r.at[0], dp=1 - d)
    du.start()

    forward(xa, 0, ua)
    h = low_of(xa, 0)
    for c in range(S):
        hop_c(("a", c)).wait_recv()
    forward(xa, 1, ua)
    h = h + low_of(xa, 1)
    relay(4)

    for n in range(parts):
        o_send[n] = partial(1, n).astype(BF16)
        o_copy(n).start()
    for n in range(parts):
        own[n] = partial(0, n) + dot_nt(lg[...], dn[0, pl.ds(n * part, part), :])

    forward(xa, 2, ua)
    h = h + low_of(xa, 2)
    for c in range(S):
        hop_f(("a", c)).wait_recv()
    forward(xa, 3, ua)
    h = h + low_of(xa, 3)
    ha[...] = h.astype(BF16)

    def out_body(n, carry):
        at = pl.ds(pl.multiple_of(n * tile, tile), tile)
        value, unused = gelu_pair(ua[n] + dot_nn(ha[...], upv[:, at]))
        base = xa[0, :, :, at].reshape(rows, tile).astype(F32)
        out_f[:, at] = (base + value).astype(BF16)
        return carry
    lax.fori_loop(0, tiles, out_body, 0)

    for k in range(S):
        hop_x(k).wait_recv()
    dd.wait_recv()
    here = dot_tn(xb[0].reshape(rows, cols), lg[...]).astype(BF16)
    there = dot_tn(xo[...].reshape(rows, cols), lg_in[...]).astype(BF16)
    out_d[...] = (here.astype(F32) + there.astype(F32)).astype(BF16)

    du.wait_recv()
    out_u[...] = (du_send[...].astype(F32) + du_recv[...].astype(F32)).astype(BF16)

    for n in range(parts):
        o_copy(n).wait_recv()
        q_copy(n).wait_recv()
        at = pl.ds(n * part, part)
        total = own[n] + o_recv[n].astype(F32) + q_recv[n].astype(F32)
        out_b[:, at] = (g[:, :, at].reshape(rows, part).astype(F32) + total).astype(BF16)

    def drain(v):
        for k in range(S):
            if k != v:
                ex(v, k).wait_send()
        if v < S - 1:
            for c in range(S):
                az(v, c).wait_send()
        if v > 0:
            gz.wait_send()
    per_section(drain)
    for k in range(S):
        hop_x(k).wait_send()
        for item in (("b", k), ("a", k)):
            hop_y(item).wait_send()
            hop_c(item).wait_send()
            hop_f(item).wait_send()
    low_copy.wait_send()
    pair_copy.wait_send()
    for n in range(parts):
        p_copy(n).wait_send()
        q_copy(n).wait_send()
        o_copy(n).wait_send()
    du.wait_send()
    dd.wait_send()


def fused_on_device(sent, stash, table, embedded, loss, weight, down, up):
    S = lax.axis_size("section")
    piece, cols = stash.shape[1], stash.shape[2]
    rows, rank = S * piece, up.shape[1]
    tile = next(k for k in (768, 512, 256, 128) if cols % k == 0)
    part = next(k for k in (384, 256, 128) if cols % k == 0)
    tiles, parts = cols // tile, cols // part
    hbm = pl.BlockSpec(memory_space=pltpu.HBM)
    vmem = pl.BlockSpec(memory_space=pltpu.VMEM)
    smem = pl.BlockSpec(memory_space=pltpu.SMEM)
    V = pltpu.VMEM
    dma = lambda *shape: pltpu.SemaphoreType.DMA(shape)
    block = (tiles, rows, tile)
    cut = (parts, rows, part)
    slim = V((rows, rank), BF16)
    stack = V((S, piece, cols), BF16)
    outs = pl.pallas_call(
        functools.partial(window_kernel, S, tile, part),
        out_shape=(
            jax.ShapeDtypeStruct((rows, cols), BF16),
            jax.ShapeDtypeStruct((rows, cols), BF16),
            jax.ShapeDtypeStruct((cols, rank), BF16),
            jax.ShapeDtypeStruct((rank, cols), BF16),
        ),
        in_specs=[hbm, hbm, smem, hbm, hbm, hbm, hbm, hbm],
        out_specs=(vmem,) * 4,
        scratch_shapes=[
            stack, V((4, cols, cols), BF16), V((4, cols, rank), BF16), V((rank, cols), BF16),
            V((4, S, piece, cols), BF16), V((4, S, piece, cols), BF16),
            stack, stack,
            V(block, F32), V(block, F32), V((rows, cols), BF16),
            slim, slim, slim, slim, slim, slim, slim, slim,
            V(cut, BF16), V(cut, BF16), V(cut, BF16),
            V(cut, BF16), V(cut, BF16), V(cut, BF16), V(cut, F32),
            V((rank, cols), BF16), V((rank, cols), BF16), stack,
            dma(4), dma(4), dma(4), dma(S), dma(S), dma(S), dma(S), dma(1), dma(1), dma(S), dma(S),
            dma(2 * S), dma(2 * S), dma(2 * S), dma(2 * S), dma(2 * S), dma(2 * S), dma(2), dma(2),
            dma(parts), dma(parts), dma(parts), dma(parts), dma(parts), dma(parts),
            dma(2), dma(2),
        ],
        compiler_params=pltpu.CompilerParams(
            collective_id=0, has_side_effects=True, vmem_limit_bytes=60 * 1024 * 1024),
    )(
        sent.reshape(2, S, piece, cols), stash, table,
        embedded.reshape(S, piece, cols), loss.reshape(S, piece, cols),
        weight.reshape(4, cols, cols), down.reshape(4, cols, rank), up[0],
    )
    return tuple(o[None] for o in outs)


def solution(mesh):
    placed = (
        P("section", "dp", "tensor"),
        P("section", "dp", "tensor"),
        P("section", None),
        P("dp", "tensor"),
        P("dp", "tensor"),
        P("section", None, "tensor"),
        P("section", None, None),
        P("section", None, "tensor"),
    )
    def program(*args):
        rows = args[1].shape[1] // mesh.shape["dp"]
        cols = args[1].shape[2] // mesh.shape["tensor"]
        fits = (
            mesh.shape["tensor"] == 4 and mesh.shape["dp"] == 2
            and rows % 16 == 0 and cols % 128 == 0
        )
        return sharded(fused_on_device if fits else on_device)(*args)

    def sharded(body):
      return jax.shard_map(
        body,
        mesh=mesh,
        in_specs=placed,
        out_specs=(
            P("section", "dp", "tensor"),
            P("section", "dp", "tensor"),
            P("section", "tensor", None),
            P("section", None, "tensor"),
        ),
        check_vma=False,
    )

    return program
```

time: 65.5 us -> 63.9 us (0.976)
  the two profiles are of different devices: /device:TPU:22 before, /device:TPU:24 now
where the time goes in v1:
time: 63.9 us; the launch traced here: 63.7 us
  Pallas kernels  58.7 us (92%)
  local copies, waits for them, and re-layouts  4.34 us (7%)
  between operations  0.67 us (1%)
    pallas_call x1, Pallas kernels, fused_on_device(): pl.pallas_call(functools.partial(window_kernel, S, tile, part), out_shape...  58.7 us
    unnamed x10, local copies, waits for them, and re-layouts  4.34 us

profile of v1, /device:TPU:24, one launch (start us, length us, event | category | flops | bytes accessed | tf_op | source)
XLA Modules:
  0.0 63.7 jit_solution(10680304894218343988)
XLA Ops:
  0.6 58.7 %shard_map.111 = (bf16[192,1536]{1,0:T(8,128)(2,1)}, bf16[192,1536]{1,0:T(8,128)(2,1)}, bf16[1536,128]{1,0:T(8,128)(2,1)}, bf16[128,1536]{1,0:T(8,128)(2,1)}) custom-call(bf16[2,4,48,1536]{3,2,1,0:T(8,128)(2,1)} %bitcast.12, bf16[4,48,1536]{2,1,0:T(8,128)(2,1)} %stash_hbm.1, s32[1,4]{1,0:T(1,128)} %table.1, bf16[4,48,1536]{2,1,0:T(8,128)(2,1)} %bitcast.13, ...), custom_call_target="tpu_custom_call" | custom-call | tf_op jit(solution)/shard_map/pallas_call | solution.py:491
  59.4 0.0 copy-start
  59.4 0.0 copy-start.2
  59.4 0.0 copy-start.1
  59.4 2.0 %copy.16 = bf16[1,192,1536]{2,1,0:T(8,128)(2,1)} copy(bf16[1,192,1536]{2,1,0:T(8,128)(2,1)} %bitcast.16) | data formatting | bytes 1179648
  61.4 0.0 copy-done
  61.4 0.8 %copy.17 = bf16[1,192,1536]{2,1,0:T(8,128)(2,1)} copy(bf16[1,192,1536]{2,1,0:T(8,128)(2,1)S(1)} %bitcast.15) | data formatting | bytes 1179648
  62.2 0.0 copy-done.2
  62.2 0.7 %copy.18 = bf16[1,1536,128]{2,1,0:T(8,128)(2,1)} copy(bf16[1,1536,128]{2,1,0:T(8,128)(2,1)S(1)} %bitcast.18) | data formatting | bytes 786432
  63.0 0.0 copy-done.1
  63.0 0.7 %copy.19 = bf16[1,128,1536]{2,1,0:T(8,128)(2,1)} copy(bf16[1,128,1536]{2,1,0:T(8,128)(2,1)S(1)} %bitcast.17) | data formatting | bytes 786432
Async XLA Ops:
  59.4 2.1 %copy-start = (bf16[192,1536]{1,0:T(8,128)(2,1)S(1)}, bf16[192,1536]{1,0:T(8,128)(2,1)}, u32[]{:S(2)}) copy-start(bf16[192,1536]{1,0:T(8,128)(2,1)} %get-tuple-element.9) | copy-start | bytes 1769476
  59.4 2.9 %copy-start.2 = (bf16[1536,128]{1,0:T(8,128)(2,1)S(1)}, bf16[1536,128]{1,0:T(8,128)(2,1)}, u32[]{:S(2)}) copy-start(bf16[1536,128]{1,0:T(8,128)(2,1)} %get-tuple-element.10) | copy-start | bytes 1179652
  59.4 3.6 %copy-start.1 = (bf16[128,1536]{1,0:T(8,128)(2,1)S(1)}, bf16[128,1536]{1,0:T(8,128)(2,1)}, u32[]{:S(2)}) copy-start(bf16[128,1536]{1,0:T(8,128)(2,1)} %get-tuple-element.11) | copy-start | bytes 1179652

commit v2 on v1

--- a/solution.py
+++ b/solution.py
@@ -116,63 +116,97 @@
 
 
 def link_order(s, S):
-    b = [("b", k) for k in stash_order(s, S)]
-    a = [("a", c) for c in range(S)]
-    if s == 0:
-        mixed = [b[0]]
-        for k in range(1, S):
-            mixed += [a[k - 1], b[k]]
-        return mixed + a[S - 1:]
-    if s == S - 1:
-        return b[:2] + a[:S - 1] + b[2:] + a[S - 1:]
-    return b + a
-
-
-def up_order(s, S):
-    b = [("b", k) for k in range(s + 1, S)]
-    a = [("a", c) for c in range(S)] if s < S - 1 else []
-    if 0 < s < S - 2:
-        return b[:1] + a[:2] + b[1:] + a[2:]
-    return b + a
-
-
-def relay_slots(s, S):
-    order = link_order(s, S)
-    last_b = max(i for i, item in enumerate(order) if item[0] == "b")
-    slots = [[], [], [], []]
-    for i in range(last_b + 1):
-        slots[0].append(("p", order[i]))
-        if i:
-            slots[0].append(("q", order[i - 1]))
-    rest = order[last_b + 1:]
-    now = len(rest) if s == 0 else 1
-    slots[1] += [("p", item) for item in rest[:now]]
-    slots[1].append(("q", order[last_b]))
-    sent = rest[:now]
-    late = []
-    for item in rest[now:]:
-        if 0 < s < S - 1 and s != 1 and item == rest[-1]:
-            late.append(item)
-            continue
-        slots[2].append(("p", item))
-        slots[2].append(("q", sent.pop(0)))
-        sent.append(item)
-    slots[3] += [("p", item) for item in late]
-    tail = [("q", item) for item in sent + late]
-    return slots + [tail]
+    return [("b", k) for k in stash_order(s, S)] + [("a", c) for c in range(S)]
+
+
+FOUR = {
+    0: {
+        0: ("a0", "~b1", "+b2", "b0'", "b1", "~b2", "+b3", "+a0", "a0'", "b1'", "a1", "+a1", "b2", "+a2", "b3",),
+        1: ("b2'", "+a3",),
+        2: ("b3'", "a2",),
+        3: ("a3",),
+        9: ("a1'",),
+        10: ("a2'", "a3'",),
+    },
+    1: {
+        0: ("~b2", "+b3", "b0", "b1'", "b2", "+g", "b0'", "+a0", "b3",),
+        1: ("b2'", "+a1", "a0",),
+        2: ("b3'", "+a2",),
+        3: ("a1", "+a3",),
+        5: ("a2", "a0'",),
+        6: ("a3", "a1'",),
+        9: ("a2'",),
+        10: ("a3'",),
+    },
+    2: {
+        0: ("~b3", "+a0", "~b1", "+b0", "b3", "b2'", "b1", "+g", "b3'", "b0", "+a1",),
+        1: ("b1'", "+a2",),
+        2: ("b0'", "+a3",),
+        3: ("a0",),
+        5: ("a1",),
+        6: ("a0'",),
+        7: ("a2",),
+        8: ("a3",),
+        9: ("a1'",),
+        10: ("a2'",),
+        11: ("a3'",),
+    },
+    3: {
+        0: ("~b2", "+b1", "b3'", "b2", "+b0", "+g", "a0", "b2'", "b1", "a0'", "b0",),
+        1: ("b1'",),
+        2: ("b0'", "a1",),
+        3: ("a2",),
+        5: ("a3",),
+        9: ("a1'",),
+        10: ("a2'",),
+        11: ("a3'",),
+    },
+}
+
+
+def read_plan(words):
+    plan = []
+    for word in words:
+        kind = "s" if word[0] == "+" else "w" if word[0] == "~" else "q" if word[-1] == "'" else "p"
+        name = word.strip("+~'")
+        plan.append((kind, (name[0], int(name[1:] or 0))))
+    return plan
+
+
+def first_targets(s, S):
+    order = stash_order(s, S)[1:]
+    held = [item[1] for kind, item in relay_slot(s, S, 0) if kind == "s" and item[0] == "b"]
+    return [k for k in order if k not in held]
+
+
+def relay_slot(s, S, slot):
+    if S == 4:
+        return read_plan(FOUR[s].get(slot, ()))
+    order = link_order(s, S)[1:]
+    if slot == 0:
+        late = [("s", ("a", c)) for c in range(S) if s < S - 1] + [("s", ("g", 0))] * (s > 0)
+        return [("p", item) for item in order if item[0] == "b"] + late
+    if slot == 2:
+        return [("q", ("b", k)) for k in range(S)]
+    if slot == 5:
+        return [(kind, item) for item in order if item[0] == "a" for kind in "pq"]
+    return []
 
 
 def window_kernel(
     sections, tile, part,
     sent, stash_hbm, table, embedded, loss, weight, down, up,
+    keep_f, keep_b, keep_d, keep_u,
     out_f, out_b, out_d, out_u,
-    stash_v, w, dn, upv, xa, xb, g, arranged, u, ua, scaled, low, low_in, pair, pair_in, lg, lg_in, hb, ha,
-    p_send, q_send, o_send, p_recv, q_recv, o_recv, own,
+    stash_v, w, dn, upv, xab, g, arranged, u, ua, scaled, low, low_in, pair, pair_in, lg, lg_in, hb, ha,
+    pqo_send, p_recv, q_recv, o_recv, own,
     du_send, du_recv, xo,
-    w_sem, d_sem, loc_sem, ex_s, ex_r, az_s, az_r, gz_s, gz_r,
-    xo_s, xo_r, y_s, y_r, c_s, c_r, f_s, f_r, low_s, low_r, p_s, p_r, q_s, q_r, o_s, o_r, dp_s, dp_r,
+    w_sem, d_sem, loc_sem, keep_sem, ex_s, ex_r, az_s, az_r, gz_s, gz_r,
+    xo_s, xo_r, hop_s, y_r, c_r, f_r, low_s, low_r, pqo_s, p_r, q_r, o_r, dp_s, dp_r,
 ):
     S = sections
+    xa, xb = xab.at[0], xab.at[1]
+    p_send, q_send, o_send = pqo_send.at[0], pqo_send.at[1], pqo_send.at[2]
     s = lax.axis_index("section")
     d = lax.axis_index("dp")
     t = lax.axis_index("tensor")
@@ -196,7 +230,8 @@
     loss_copy = pltpu.make_async_copy(loss, g, loc_sem.at[1])
     up_copy = pltpu.make_async_copy(up, upv, loc_sem.at[2])
     w_copies = [pltpu.make_async_copy(weight.at[rel[r]], w.at[r], w_sem.at[r]) for r in range(4)]
-    d_copies = [pltpu.make_async_copy(down.at[rel[r]], dn.at[r], d_sem.at[r]) for r in range(4)]
+    d_copies = [pltpu.make_async_copy(down.at[rel[r]], dn.at[r], d_sem.at[0]) for r in range(4)]
+    d_all = pltpu.make_async_copy(down, dn, d_sem.at[0])
 
     barrier = pltpu.get_barrier_semaphore()
     for j in range(1, S):
@@ -225,27 +260,43 @@
         return remote(arranged.at[(to - v) % S], xb.at[0, v], ex_s.at[to], ex_r.at[v], section=to)
 
     def az(v, c):
-        return remote(sent.at[1, c], xa.at[0, c], az_s.at[c], az_r.at[c], section=(v + 1) % S)
+        return remote(sent.at[1, c], xa.at[0, c], az_s.at[0], az_r.at[c], section=(v + 1) % S)
 
     gz = remote(sent.at[0], g, gz_s.at[0], gz_r.at[0], section=(s + S - 1) % S)
 
+    def place(item):
+        kind = 1 if item[0] == "b" else 0
+        return (xb if kind else xa), item[1], kind
+
     def hop_y(item):
-        x, k, at = (xb, item[1], item[1]) if item[0] == "b" else (xa, item[1], S + item[1])
-        return remote(x.at[0, k], x.at[2, k], y_s.at[at], y_r.at[at], tensor=t2)
+        x, k, kind = place(item)
+        return remote(x.at[0, k], x.at[2, k], hop_s.at[0], y_r.at[kind * S + k], tensor=t2)
 
     def hop_c(item):
-        x, k, at = (xb, item[1], item[1]) if item[0] == "b" else (xa, item[1], S + item[1])
-        return remote(x.at[0, k], x.at[1, k], c_s.at[at], c_r.at[at], tensor=t1)
+        x, k, kind = place(item)
+        return remote(x.at[0, k], x.at[1, k], hop_s.at[0], c_r.at[kind], tensor=t1)
 
     def hop_f(item):
-        x, k, at = (xb, item[1], item[1]) if item[0] == "b" else (xa, item[1], S + item[1])
-        return remote(x.at[2, k], x.at[3, k], f_s.at[at], f_r.at[at], tensor=t1)
+        x, k, kind = place(item)
+        return remote(x.at[2, k], x.at[3, k], hop_s.at[0], f_r.at[kind], tensor=t1)
+
+    def all_c(x, kind):
+        return remote(x.at[0], x.at[1], hop_s.at[0], c_r.at[kind], tensor=t1)
+
+    def all_f(x, kind):
+        return remote(x.at[2], x.at[3], hop_s.at[0], f_r.at[kind], tensor=t1)
 
     def hop_x(k):
-        return remote(xb.at[0, k], xo.at[k], xo_s.at[k], xo_r.at[k], dp=1 - d)
+        return remote(xb.at[0, k], xo.at[k], xo_s.at[0], xo_r.at[0], dp=1 - d)
+
+    all_x = remote(xb.at[0], xo, xo_s.at[0], xo_r.at[0], dp=1 - d)
 
     def act(v, step):
         kind, item = step
+        if kind in "sw":
+            copy = gz if item[0] == "g" else az(v, item[1]) if item[0] == "a" else ex(v, item[1])
+            copy.start() if kind == "s" else copy.wait_send()
+            return
         if kind == "q":
             hop_y(item).wait_recv()
             hop_f(item).start()
@@ -269,21 +320,14 @@
 
     def relay(slot):
         def run(v):
-            for step in relay_slots(v, S)[slot]:
+            for step in relay_slot(v, S, slot):
                 act(v, step)
         per_section(run)
 
     def first_sends(v):
         act(v, ("p", ("b", v)))
-        for k in range(v - 1, -1, -1):
+        for k in first_targets(v, S):
             ex(v, k).start()
-        for kind, k in up_order(v, S):
-            if kind == "b":
-                ex(v, k).start()
-            else:
-                az(v, k).start()
-        if v > 0:
-            gz.start()
         if v == S - 1:
             loss_copy.start()
     per_section(first_sends)
@@ -294,7 +338,7 @@
     up_copy.start()
 
     def run_rest(v):
-        for step in relay_slots(v, S)[0][1:]:
+        for step in relay_slot(v, S, 0):
             act(v, step)
     per_section(run_rest)
 
@@ -306,28 +350,26 @@
     def low_of(x, r):
         return dot_nn(x[r].reshape(rows, cols), dn[r])
 
-    d_copies[0].wait()
+    d_all.wait()
     w_copies[0].wait()
     forward(xb, 0, u)
     h = low_of(xb, 0)
-    for k in range(S):
-        hop_c(("b", k)).wait_recv()
-    d_copies[1].wait()
+    relay(1)
+    all_c(xb, 1).wait_recv()
     w_copies[1].wait()
     forward(xb, 1, u)
     h = h + low_of(xb, 1)
-    relay(1)
-    d_copies[2].wait()
+    relay(2)
     w_copies[2].wait()
     forward(xb, 2, u)
     h = h + low_of(xb, 2)
-    for k in range(S):
-        hop_f(("b", k)).wait_recv()
-    d_copies[3].wait()
+    relay(3)
+    all_f(xb, 1).wait_recv()
     w_copies[3].wait()
     forward(xb, 3, u)
     h = h + low_of(xb, 3)
     hb[...] = h.astype(BF16)
+    relay(4)
     up_copy.wait()
 
     def slope_body(n, carry):
@@ -336,7 +378,16 @@
         u[n] = slope
         return carry
     lax.fori_loop(0, tiles, slope_body, 0)
-    relay(2)
+    relay(5)
+    relay(6)
+
+    def near_blocks():
+        forward(xa, 0, ua)
+        all_c(xa, 0).wait_recv()
+        forward(xa, 1, ua)
+    early = (s > 0) & (s < S // 2)
+    pl.when(early)(near_blocks)
+    relay(7)
 
     @pl.when(s == S - 1)
     def _():
@@ -353,70 +404,85 @@
     lax.fori_loop(0, tiles, scale_body, 0)
 
     low_copy = remote(low, low_in, low_s.at[0], low_r.at[0], tensor=t1)
-    pair_copy = remote(pair, pair_in, low_s.at[1], low_r.at[1], tensor=t2)
+    share = rows // 2
+    lower = pl.ds(pl.multiple_of((t % 2) * share, share), share)
+    pair_copy = remote(pair.at[lower], pair_in.at[lower], low_s.at[1], low_r.at[1], tensor=t2)
+    pair_hop = remote(pair_in.at[lower], pair_in.at[lower], low_s.at[2], low_r.at[2], tensor=t1)
 
     def partial(r, n):
         return dot_nt(scaled[...], w[r, pl.ds(n * part, part), :])
 
     def p_copy(n):
-        return remote(p_send.at[n], p_recv.at[n], p_s.at[n], p_r.at[n], tensor=t1)
+        return remote(p_send.at[n], p_recv.at[n], pqo_s.at[0], p_r.at[(n >= lead) + (n >= parts - lead)], tensor=t1)
+
+    def p_group(group):
+        at = pl.ds(group[0], len(group))
+        which = (group[0] >= lead) + (group[0] >= parts - lead)
+        return remote(p_send.at[at], p_recv.at[at], pqo_s.at[0], p_r.at[which], tensor=t1)
 
     def q_copy(n):
-        return remote(q_send.at[n], q_recv.at[n], q_s.at[n], q_r.at[n], tensor=t2)
+        return remote(q_send.at[n], q_recv.at[n], pqo_s.at[0], q_r.at[n], tensor=t2)
 
     def o_copy(n):
-        return remote(o_send.at[n], o_recv.at[n], o_s.at[n], o_r.at[n], tensor=t1)
-
-    def p_step(n):
-        p_send[n] = partial(3, n).astype(BF16)
-        p_copy(n).start()
-
-    def q_step(n):
-        mine = partial(2, n)
-        p_copy(n).wait_recv()
-        q_send[n] = (mine + p_recv[n].astype(F32)).astype(BF16)
-        q_copy(n).start()
-
+        return remote(o_send.at[n], o_recv.at[n], pqo_s.at[0], o_r.at[0], tensor=t1)
+
+    lead = max(parts // 4, 1)
+    first, second, third = range(lead), range(lead, parts - lead), range(parts - lead, parts)
+
+    def p_step(group):
+        for n in group:
+            p_send[n] = partial(3, n).astype(BF16)
+        for n in group:
+            p_copy(n).start()
+
+    def q_step(group):
+        for n in group:
+            own[n] = partial(2, n)
+        p_group(group).wait_recv()
+        for n in group:
+            q_send[n] = (own[n] + p_recv[n].astype(F32)).astype(BF16)
+        for n in group:
+            q_copy(n).start()
+
+    p_step(first)
     low[...] = dot_nt(scaled[...], upv[...]).astype(BF16)
     low_copy.start()
-    p_step(0)
-    p_step(1)
+    relay(8)
+    q_step(first)
+    relay(9)
+    p_step(second)
+    du_send[...] = dot_tn(hb[...], scaled[...]).astype(BF16)
+    du = remote(du_send, du_recv, dp_s.at[0], dp_r.at[0], dp=1 - d)
+    du.start()
     low_copy.wait_recv()
     pair[...] = (low[...].astype(F32) + low_in[...].astype(F32)).astype(BF16)
     pair_copy.start()
-    q_step(0)
-    relay(3)
-    for n in range(2, parts):
-        p_step(n)
-        q_step(n - 1)
-    q_step(parts - 1)
-
-    du_send[...] = dot_tn(hb[...], scaled[...]).astype(BF16)
+    relay(12)
+
+    def o_step(group):
+        for n in group:
+            o_send[n] = partial(1, n).astype(BF16)
+        for n in group:
+            o_copy(n).start()
+
+    o_step(range(parts // 2))
+    q_step(second)
+    p_step(third)
+    pl.when(jnp.logical_not(early))(near_blocks)
+    relay(10)
+    q_step(third)
+    o_step(range(parts // 2, parts))
+    relay(11)
     pair_copy.wait_recv()
+    pair_hop.start()
+    h = low_of(xa, 0) + low_of(xa, 1)
+    forward(xa, 2, ua)
+    h = h + low_of(xa, 2)
+    pair_hop.wait_recv()
     lg[...] = (pair[...].astype(F32) + pair_in[...].astype(F32)).astype(BF16)
     dd = remote(lg, lg_in, dp_s.at[1], dp_r.at[1], dp=1 - d)
     dd.start()
-    du = remote(du_send, du_recv, dp_s.at[0], dp_r.at[0], dp=1 - d)
-    du.start()
-
-    forward(xa, 0, ua)
-    h = low_of(xa, 0)
-    for c in range(S):
-        hop_c(("a", c)).wait_recv()
-    forward(xa, 1, ua)
-    h = h + low_of(xa, 1)
-    relay(4)
-
-    for n in range(parts):
-        o_send[n] = partial(1, n).astype(BF16)
-        o_copy(n).start()
-    for n in range(parts):
-        own[n] = partial(0, n) + dot_nt(lg[...], dn[0, pl.ds(n * part, part), :])
-
-    forward(xa, 2, ua)
-    h = h + low_of(xa, 2)
-    for c in range(S):
-        hop_f(("a", c)).wait_recv()
+    all_f(xa, 0).wait_recv()
     forward(xa, 3, ua)
     h = h + low_of(xa, 3)
     ha[...] = h.astype(BF16)
@@ -428,48 +494,63 @@
         out_f[:, at] = (base + value).astype(BF16)
         return carry
     lax.fori_loop(0, tiles, out_body, 0)
-
-    for k in range(S):
-        hop_x(k).wait_recv()
-    dd.wait_recv()
-    here = dot_tn(xb[0].reshape(rows, cols), lg[...]).astype(BF16)
-    there = dot_tn(xo[...].reshape(rows, cols), lg_in[...]).astype(BF16)
-    out_d[...] = (here.astype(F32) + there.astype(F32)).astype(BF16)
+    keeps = [
+        pltpu.make_async_copy(out_f, keep_f, keep_sem.at[0]),
+        pltpu.make_async_copy(out_u, keep_u, keep_sem.at[1]),
+        pltpu.make_async_copy(out_d, keep_d, keep_sem.at[2]),
+    ]
+    keeps[0].start()
+
+    for n in range(parts):
+        own[n] = partial(0, n) + dot_nt(lg[...], dn[0, pl.ds(n * part, part), :])
 
     du.wait_recv()
     out_u[...] = (du_send[...].astype(F32) + du_recv[...].astype(F32)).astype(BF16)
-
+    keeps[1].start()
+
+    all_x.wait_recv()
+    dd.wait_recv()
+    here = dot_tn(lg[...], xb[0].reshape(rows, cols))
+    there = dot_tn(lg_in[...], xo[...].reshape(rows, cols))
+    out_d[...] = (here + there).T.astype(BF16)
+    keeps[2].start()
+
+    remote(o_send, o_recv, pqo_s.at[0], o_r.at[0], tensor=t1).wait_recv()
     for n in range(parts):
-        o_copy(n).wait_recv()
         q_copy(n).wait_recv()
         at = pl.ds(n * part, part)
         total = own[n] + o_recv[n].astype(F32) + q_recv[n].astype(F32)
         out_b[:, at] = (g[:, :, at].reshape(rows, part).astype(F32) + total).astype(BF16)
+        pltpu.make_async_copy(out_b.at[:, at], keep_b.at[:, at], keep_sem.at[3]).start()
 
     def drain(v):
         for k in range(S):
-            if k != v:
+            if k != v and ("w", ("b", k)) not in relay_slot(v, S, 0):
                 ex(v, k).wait_send()
         if v < S - 1:
-            for c in range(S):
-                az(v, c).wait_send()
+            remote(sent.at[1], xa.at[0], az_s.at[0], az_r.at[0], section=v + 1).wait_send()
         if v > 0:
             gz.wait_send()
     per_section(drain)
-    for k in range(S):
-        hop_x(k).wait_send()
-        for item in (("b", k), ("a", k)):
-            hop_y(item).wait_send()
-            hop_c(item).wait_send()
-            hop_f(item).wait_send()
+    all_x.wait_send()
+    remote(xab.at[:, 0:3], xab.at[:, 1:4], hop_s.at[0], y_r.at[0], tensor=t1).wait_send()
     low_copy.wait_send()
     pair_copy.wait_send()
-    for n in range(parts):
-        p_copy(n).wait_send()
-        q_copy(n).wait_send()
-        o_copy(n).wait_send()
+    pair_hop.wait_send()
+    remote(pqo_send, pqo_send, pqo_s.at[0], p_r.at[0], tensor=t1).wait_send()
     du.wait_send()
     dd.wait_send()
+    for keep in keeps:
+        keep.wait()
+    pltpu.make_async_copy(out_b, keep_b, keep_sem.at[3]).wait()
+
+
+def store_kernel(*refs):
+    copies = [pltpu.make_async_copy(refs[i], refs[4 + i], refs[8].at[i]) for i in range(4)]
+    for copy in copies:
+        copy.start()
+    for copy in copies:
+        copy.wait()
 
 
 def fused_on_device(sent, stash, table, embedded, loss, weight, down, up):
@@ -479,8 +560,8 @@
     tile = next(k for k in (768, 512, 256, 128) if cols % k == 0)
     part = next(k for k in (384, 256, 128) if cols % k == 0)
     tiles, parts = cols // tile, cols // part
+    far = lambda x: pltpu.with_memory_space_constraint(x, pltpu.HBM)
     hbm = pl.BlockSpec(memory_space=pltpu.HBM)
-    vmem = pl.BlockSpec(memory_space=pltpu.VMEM)
     smem = pl.BlockSpec(memory_space=pltpu.SMEM)
     V = pltpu.VMEM
     dma = lambda *shape: pltpu.SemaphoreType.DMA(shape)
@@ -497,29 +578,36 @@
             jax.ShapeDtypeStruct((rank, cols), BF16),
         ),
         in_specs=[hbm, hbm, smem, hbm, hbm, hbm, hbm, hbm],
-        out_specs=(vmem,) * 4,
+        out_specs=(pl.BlockSpec(memory_space=pl.ANY),) * 4,
         scratch_shapes=[
+            V((rows, cols), BF16), V((rows, cols), BF16), V((cols, rank), BF16), V((rank, cols), BF16),
             stack, V((4, cols, cols), BF16), V((4, cols, rank), BF16), V((rank, cols), BF16),
-            V((4, S, piece, cols), BF16), V((4, S, piece, cols), BF16),
+            V((2, 4, S, piece, cols), BF16),
             stack, stack,
             V(block, F32), V(block, F32), V((rows, cols), BF16),
             slim, slim, slim, slim, slim, slim, slim, slim,
-            V(cut, BF16), V(cut, BF16), V(cut, BF16),
-            V(cut, BF16), V(cut, BF16), V(cut, BF16), V(cut, F32),
+            V((3,) + cut, BF16), V(cut, BF16), V(cut, BF16), V(cut, BF16), V(cut, F32),
             V((rank, cols), BF16), V((rank, cols), BF16), stack,
-            dma(4), dma(4), dma(4), dma(S), dma(S), dma(S), dma(S), dma(1), dma(1), dma(S), dma(S),
-            dma(2 * S), dma(2 * S), dma(2 * S), dma(2 * S), dma(2 * S), dma(2 * S), dma(2), dma(2),
-            dma(parts), dma(parts), dma(parts), dma(parts), dma(parts), dma(parts),
+            dma(4), dma(1), dma(4), dma(4), dma(S), dma(S), dma(1), dma(S), dma(1), dma(1),
+            dma(1), dma(1), dma(1), dma(2 * S), dma(2), dma(2), dma(3), dma(3), dma(1), dma(3), dma(parts), dma(1),
             dma(2), dma(2),
         ],
         compiler_params=pltpu.CompilerParams(
-            collective_id=0, has_side_effects=True, vmem_limit_bytes=60 * 1024 * 1024),
+            collective_id=0, has_side_effects=True, vmem_limit_bytes=44 * 1024 * 1024),
     )(
-        sent.reshape(2, S, piece, cols), stash, table,
-        embedded.reshape(S, piece, cols), loss.reshape(S, piece, cols),
-        weight.reshape(4, cols, cols), down.reshape(4, cols, rank), up[0],
-    )
-    return tuple(o[None] for o in outs)
+        far(sent.reshape(2, S, piece, cols)), far(stash), far(table),
+        far(embedded.reshape(S, piece, cols)), far(loss.reshape(S, piece, cols)),
+        far(weight.reshape(4, cols, cols)), far(down.reshape(4, cols, rank)), far(up[0]),
+    )
+    stored = pl.pallas_call(
+        store_kernel,
+        out_shape=tuple(jax.ShapeDtypeStruct(o.shape, o.dtype) for o in outs),
+        in_specs=[pl.BlockSpec(memory_space=pl.ANY)] * 4,
+        out_specs=(hbm,) * 4,
+        scratch_shapes=[dma(4)],
+        compiler_params=pltpu.CompilerParams(vmem_limit_bytes=1024 * 1024),
+    )(*outs)
+    return tuple(o[None] for o in stored)
 
 
 def solution(mesh):

time: 63.9 us -> 52.6 us (0.82)
  the two profiles are of different devices: /device:TPU:24 before, /device:TPU:0 now
where the time goes in v2:
time: 52.6 us; the launch traced here: 52.4 us
  Pallas kernels  51.6 us (98%)
  between operations  0.8 us (2%)
    pallas_call x1, Pallas kernels, fused_on_device(): pl.pallas_call(functools.partial(window_kernel, S, tile, part), out_shape...  50.3 us
    pallas_call x1, Pallas kernels, fused_on_device(): pl.pallas_call(store_kernel, out_shape=tuple((jax.ShapeDtypeStruct(o.shap...  1.3 us

profile of v2, /device:TPU:0, one launch (start us, length us, event | category | flops | bytes accessed | tf_op | source)
XLA Modules:
  0.0 52.4 jit_solution(1288605409143783274)
XLA Ops:
  0.6 50.3 %shard_map.111 = (bf16[192,1536]{1,0:T(8,128)(2,1)S(1)}, bf16[192,1536]{1,0:T(8,128)(2,1)S(1)}, bf16[1536,128]{1,0:T(8,128)(2,1)S(1)}, bf16[128,1536]{1,0:T(8,128)(2,1)S(1)}) custom-call(bf16[2,4,48,1536]{3,2,1,0:T(8,128)(2,1)} %bitcast.12, bf16[4,48,1536]{2,1,0:T(8,128)(2,1)} %stash_hbm.1, s32[1,4]{1,0:T(1,128)} %table.1, bf16[4,48,1536]{2,1,0:T(8,128)(2,1)} %bitcast.13, ...), custom_call_target="tpu_custom_call" | custom-call | tf_op jit(solution)/shard_map/pallas_call | solution.py:572
  51.0 1.3 %shard_map.112 = (bf16[192,1536]{1,0:T(8,128)(2,1)}, bf16[192,1536]{1,0:T(8,128)(2,1)}, bf16[1536,128]{1,0:T(8,128)(2,1)}, bf16[128,1536]{1,0:T(8,128)(2,1)}) custom-call(bf16[192,1536]{1,0:T(8,128)(2,1)S(1)} %get-tuple-element.12.refs_0_, bf16[192,1536]{1,0:T(8,128)(2,1)S(1)} %get-tuple-element.13.refs_1_, bf16[1536,128]{1,0:T(8,128)(2,1)S(1)} %get-tuple-element.14.refs_2_, ...), custom_call_target="tpu_custom_call" | custom-call | tf_op jit(solution)/shard_map/pallas_call | solution.py:602

commit v3 on v2

--- a/solution.py
+++ b/solution.py
@@ -129,22 +129,22 @@
         10: ("a2'", "a3'",),
     },
     1: {
-        0: ("~b2", "+b3", "b0", "b1'", "b2", "+g", "b0'", "+a0", "b3",),
-        1: ("b2'", "+a1", "a0",),
-        2: ("b3'", "+a2",),
+        0: ("~b2", "+b3", "b0", "b1'", "b2", "+g", "+a0", "b0'", "b3",),
+        1: ("+a1", "b2'", "a0",),
+        2: ("+a2", "b3'",),
         3: ("a1", "+a3",),
-        5: ("a2", "a0'",),
-        6: ("a3", "a1'",),
+        4: ("a2",),
+        5: ("a0'", "a3",),
+        6: ("a1'",),
         9: ("a2'",),
         10: ("a3'",),
     },
     2: {
         0: ("~b3", "+a0", "~b1", "+b0", "b3", "b2'", "b1", "+g", "b3'", "b0", "+a1",),
         1: ("b1'", "+a2",),
-        2: ("b0'", "+a3",),
-        3: ("a0",),
-        5: ("a1",),
-        6: ("a0'",),
+        2: ("b0'", "+a3", "a0",),
+        4: ("a1",),
+        5: ("a0'",),
         7: ("a2",),
         8: ("a3",),
         9: ("a1'",),
@@ -195,10 +195,10 @@
 
 def window_kernel(
     sections, tile, part,
-    sent, stash_hbm, table, embedded, loss, weight, down, up,
+    sent, stash_hbm, table_hbm, embedded, loss, weight, down, up,
     keep_f, keep_b, keep_d, keep_u,
     out_f, out_b, out_d, out_u,
-    stash_v, w, dn, upv, xab, g, arranged, u, ua, scaled, low, low_in, pair, pair_in, lg, lg_in, hb, ha,
+    table, stash_v, w, dn, upv, xab, g, arranged, u, ua, scaled, low, low_in, pair, pair_in, lg, lg_in, hb, ha,
     pqo_send, p_recv, q_recv, o_recv, own,
     du_send, du_recv, xo,
     w_sem, d_sem, loc_sem, keep_sem, ex_s, ex_r, az_s, az_r, gz_s, gz_r,
@@ -220,6 +220,8 @@
     parts = cols // part
     stash_copy = pltpu.make_async_copy(stash_hbm, stash_v, loc_sem.at[0])
     stash_copy.start()
+    table_copy = pltpu.make_async_copy(table_hbm, table, loc_sem.at[4])
+    table_copy.start()
 
     def remote(src, dst, ss, rs, **device):
         return pltpu.make_async_remote_copy(
@@ -244,6 +246,7 @@
     def _():
         emb_copy.start()
 
+    table_copy.wait()
     stash_copy.wait()
     for j in range(S):
         dest = (s + j) % S
@@ -562,7 +565,6 @@
     tiles, parts = cols // tile, cols // part
     far = lambda x: pltpu.with_memory_space_constraint(x, pltpu.HBM)
     hbm = pl.BlockSpec(memory_space=pltpu.HBM)
-    smem = pl.BlockSpec(memory_space=pltpu.SMEM)
     V = pltpu.VMEM
     dma = lambda *shape: pltpu.SemaphoreType.DMA(shape)
     block = (tiles, rows, tile)
@@ -577,18 +579,18 @@
             jax.ShapeDtypeStruct((cols, rank), BF16),
             jax.ShapeDtypeStruct((rank, cols), BF16),
         ),
-        in_specs=[hbm, hbm, smem, hbm, hbm, hbm, hbm, hbm],
+        in_specs=[hbm, hbm, hbm, hbm, hbm, hbm, hbm, hbm],
         out_specs=(pl.BlockSpec(memory_space=pl.ANY),) * 4,
         scratch_shapes=[
             V((rows, cols), BF16), V((rows, cols), BF16), V((cols, rank), BF16), V((rank, cols), BF16),
-            stack, V((4, cols, cols), BF16), V((4, cols, rank), BF16), V((rank, cols), BF16),
+            pltpu.SMEM(table.shape, table.dtype), stack, V((4, cols, cols), BF16), V((4, cols, rank), BF16), V((rank, cols), BF16),
             V((2, 4, S, piece, cols), BF16),
             stack, stack,
             V(block, F32), V(block, F32), V((rows, cols), BF16),
             slim, slim, slim, slim, slim, slim, slim, slim,
             V((3,) + cut, BF16), V(cut, BF16), V(cut, BF16), V(cut, BF16), V(cut, F32),
             V((rank, cols), BF16), V((rank, cols), BF16), stack,
-            dma(4), dma(1), dma(4), dma(4), dma(S), dma(S), dma(1), dma(S), dma(1), dma(1),
+            dma(4), dma(1), dma(5), dma(4), dma(S), dma(S), dma(1), dma(S), dma(1), dma(1),
             dma(1), dma(1), dma(1), dma(2 * S), dma(2), dma(2), dma(3), dma(3), dma(1), dma(3), dma(parts), dma(1),
             dma(2), dma(2),
         ],

time: 52.6 us -> 51.9 us (0.987)
  Pallas kernels: 51.6 us -> 51 us
    pallas_call x1, Pallas kernels: 50.3 us -> 49.6 us  [fused_on_device(): pl.pallas_call(functools.partial(window_kernel, S, tile, part), out_shape...]
where the time goes in v3:
time: 51.9 us; the launch traced here: 51.8 us
  Pallas kernels  51 us (98%)
  between operations  0.8 us (2%)
    pallas_call x1, Pallas kernels, fused_on_device(): pl.pallas_call(functools.partial(window_kernel, S, tile, part), out_shape...  49.6 us
    pallas_call x1, Pallas kernels, fused_on_device(): pl.pallas_call(store_kernel, out_shape=tuple((jax.ShapeDtypeStruct(o.shap...  1.3 us

profile of v3, /device:TPU:0, one launch (start us, length us, event | category | flops | bytes accessed | tf_op | source)
XLA Modules:
  0.0 51.8 jit_solution(10414105594516396728)
XLA Ops:
  0.6 49.6 %shard_map.111 = (bf16[192,1536]{1,0:T(8,128)(2,1)S(1)}, bf16[192,1536]{1,0:T(8,128)(2,1)S(1)}, bf16[1536,128]{1,0:T(8,128)(2,1)S(1)}, bf16[128,1536]{1,0:T(8,128)(2,1)S(1)}) custom-call(bf16[2,4,48,1536]{3,2,1,0:T(8,128)(2,1)} %bitcast.12, bf16[4,48,1536]{2,1,0:T(8,128)(2,1)} %stash_hbm.1, s32[1,4]{1,0:T(1,128)} %table_hbm.1, ...), custom_call_target="tpu_custom_call" | custom-call | tf_op jit(solution)/shard_map/pallas_call | solution.py:574
  50.3 1.3 %shard_map.112 = (bf16[192,1536]{1,0:T(8,128)(2,1)}, bf16[192,1536]{1,0:T(8,128)(2,1)}, bf16[1536,128]{1,0:T(8,128)(2,1)}, bf16[128,1536]{1,0:T(8,128)(2,1)}) custom-call(bf16[192,1536]{1,0:T(8,128)(2,1)S(1)} %get-tuple-element.12.refs_0_, bf16[192,1536]{1,0:T(8,128)(2,1)S(1)} %get-tuple-element.13.refs_1_, bf16[1536,128]{1,0:T(8,128)(2,1)S(1)} %get-tuple-element.14.refs_2_, ...), custom_call_target="tpu_custom_call" | custom-call | tf_op jit(solution)/shard_map/pallas_call | solution.py:604

commit v4 on v3

--- a/solution.py
+++ b/solution.py
@@ -520,11 +520,8 @@
 
     remote(o_send, o_recv, pqo_s.at[0], o_r.at[0], tensor=t1).wait_recv()
     for n in range(parts):
-        q_copy(n).wait_recv()
         at = pl.ds(n * part, part)
-        total = own[n] + o_recv[n].astype(F32) + q_recv[n].astype(F32)
-        out_b[:, at] = (g[:, :, at].reshape(rows, part).astype(F32) + total).astype(BF16)
-        pltpu.make_async_copy(out_b.at[:, at], keep_b.at[:, at], keep_sem.at[3]).start()
+        own[n] = own[n] + o_recv[n].astype(F32) + g[:, :, at].reshape(rows, part).astype(F32)
 
     def drain(v):
         for k in range(S):
@@ -540,6 +537,12 @@
     low_copy.wait_send()
     pair_copy.wait_send()
     pair_hop.wait_send()
+    for n in range(parts):
+        q_copy(n).wait_recv()
+        at = pl.ds(n * part, part)
+        out_b[:, at] = (own[n] + q_recv[n].astype(F32)).astype(BF16)
+        pltpu.make_async_copy(out_b.at[:, at], keep_b.at[:, at], keep_sem.at[3]).start()
+
     remote(pqo_send, pqo_send, pqo_s.at[0], p_r.at[0], tensor=t1).wait_send()
     du.wait_send()
     dd.wait_send()

time: 51.9 us -> 51.8 us (level)
  no operation moved by 1% of the time
where the time goes in v4:
time: 51.8 us; the launch traced here: 51.7 us
  Pallas kernels  50.9 us (98%)
  between operations  0.8 us (2%)
    pallas_call x1, Pallas kernels, fused_on_device(): pl.pallas_call(functools.partial(window_kernel, S, tile, part), out_shape...  49.6 us
    pallas_call x1, Pallas kernels, fused_on_device(): pl.pallas_call(store_kernel, out_shape=tuple((jax.ShapeDtypeStruct(o.shap...  1.3 us

profile of v4, /device:TPU:0, one launch (start us, length us, event | category | flops | bytes accessed | tf_op | source)
XLA Modules:
  0.0 51.7 jit_solution(14973408890049759306)
XLA Ops:
  0.6 49.6 %shard_map.111 = (bf16[192,1536]{1,0:T(8,128)(2,1)S(1)}, bf16[192,1536]{1,0:T(8,128)(2,1)S(1)}, bf16[1536,128]{1,0:T(8,128)(2,1)S(1)}, bf16[128,1536]{1,0:T(8,128)(2,1)S(1)}) custom-call(bf16[2,4,48,1536]{3,2,1,0:T(8,128)(2,1)} %bitcast.12, bf16[4,48,1536]{2,1,0:T(8,128)(2,1)} %stash_hbm.1, s32[1,4]{1,0:T(1,128)} %table_hbm.1, ...), custom_call_target="tpu_custom_call" | custom-call | tf_op jit(solution)/shard_map/pallas_call | solution.py:577
  50.2 1.3 %shard_map.112 = (bf16[192,1536]{1,0:T(8,128)(2,1)}, bf16[192,1536]{1,0:T(8,128)(2,1)}, bf16[1536,128]{1,0:T(8,128)(2,1)}, bf16[128,1536]{1,0:T(8,128)(2,1)}) custom-call(bf16[192,1536]{1,0:T(8,128)(2,1)S(1)} %get-tuple-element.12.refs_0_, bf16[192,1536]{1,0:T(8,128)(2,1)S(1)} %get-tuple-element.13.refs_1_, bf16[1536,128]{1,0:T(8,128)(2,1)S(1)} %get-tuple-element.14.refs_2_, ...), custom_call_target="tpu_custom_call" | custom-call | tf_op jit(solution)/shard_map/pallas_call | solution.py:607
